TPU v7x, 256 devices: a whole 4x4x8 slice. The times are simulated.
256 devices in a mesh: dp: 8 (over z_lo, core), expert: 32 (over x, z_hi, y).
Axes of the slice: x: 4, y: 4, z: 8 (z_hi: 2, z_lo: 4; z = z_hi * 4 + z_lo), core: 2. Of those that a mesh axis runs over, the one named last changes fastest.
Arguments:
- tokens: bfloat16 [16384, 2048], P(('dp', 'expert')), may hold values from -6 to 6
- routes: int32 [16384, 8], P(('dp', 'expert')), may hold values from 0 to 63, all different within a row; in each aligned block of 64 rows (0 to 63, 64 to 127, ...) at most 12 rows name the same one
- route_weight: int32 [16384, 8], P(('dp', 'expert')), may hold values from 1 to 65535
- capacity: int32 [64], replicated, may hold values from 8 to 10
- hot_expert: int32 [1], replicated, may hold values from 0 to 63
- w_gate: bfloat16 [64, 2048, 768], P('expert', 'dp'), may hold values from -0.125 to 0.125
- w_up: bfloat16 [64, 2048, 768], P('expert', 'dp'), may hold values from -0.125 to 0.125
- w_down: bfloat16 [64, 768, 2048], P('expert', None, 'dp'), may hold values from -0.21875 to 0.21875
Outputs:
- mixed: bfloat16 [16384, 2048], P(('dp', 'expert'))
All inputs are finite; a program needn't handle non-finite values.
Results may differ from a plain program's by a relative error of at most 0.0057.
Values may be sent and summed in bfloat16 or wider, within the bound.
No kernel may reach another device: no remote copies, remote signals or barrier semaphores. Data moves between devices by JAX's collectives and lax.ppermute only.
A program may use at most 128 MiB of HBM per device.

v0:
```python
import functools
import jax
import jax.numpy as jnp
from jax import lax
from jax.sharding import Mesh, PartitionSpec as P
from jax.experimental import pallas as pl
from jax.experimental.pallas import tpu as pltpu

SLOTS = 12
EARLY = 4
LATE = SLOTS - EARLY
DESTS = 16
TOP = 8
GRANT_UP, GRANT_DOWN, GRANT_A, GRANT_B, GRANT_C = 54, 54, 10, 10, 6
BF = jnp.bfloat16
SMEM = pl.BlockSpec(memory_space=pltpu.SMEM)
VMEM = pl.BlockSpec(memory_space=pltpu.VMEM)
ANY = pl.BlockSpec(memory_space=pl.ANY)


def grant(mib):
    return pltpu.CompilerParams(vmem_limit_bytes=mib << 20)


def pack_kernel(t_ref, r_ref, w_ref, o_ref):
    half = t_ref.shape[0] // 2
    tok = t_ref.shape[0]
    o_ref[0:half, :] = t_ref[0:half, :]
    o_ref[half + TOP :, :] = t_ref[half:, :]
    weight = w_ref[...]
    high = weight // 256
    low = weight - high * 256
    gap = jnp.zeros((TOP, 128 - tok), jnp.float32)
    parts = []
    for v in (r_ref[...], high, low):
        parts += [v.astype(jnp.float32), gap]
    used = 128 * 3
    o_ref[half : half + TOP, 0:used] = jnp.concatenate(parts, axis=1).astype(BF)
    o_ref[half : half + TOP, used:] = jnp.zeros((TOP, t_ref.shape[1] - used), BF)


def weights_kernel(s_ref, g_ref, u_ref, d_ref, mgu, ogu, md, od, bgu, bd, sem_in, sem_out):
    zp = s_ref[0]
    loads, stores = [], []
    for which in (0, 1):
        e = zp if which == 0 else 1 - zp
        gu_out, d_out = ((mgu, md), (ogu, od))[which]
        for i, src in enumerate((g_ref, u_ref)):
            loads.append(pltpu.make_async_copy(src.at[e], bgu.at[which, i], sem_in.at[which * 3 + i]))
            stores.append(
                pltpu.make_async_copy(bgu.at[which, i], gu_out.at[i], sem_out.at[which * 3 + i])
            )
        loads.append(pltpu.make_async_copy(d_ref.at[e], bd.at[which], sem_in.at[which * 3 + 2]))
        stores.append(pltpu.make_async_copy(bd.at[which], d_out, sem_out.at[which * 3 + 2]))
    for c in loads:
        c.start()
    for a, b in zip(loads, stores):
        a.wait()
        b.start()
    for b in stores:
        b.wait()


def read_meta(ref, half, tok):
    rows = ref[half : half + TOP, 0:384].astype(jnp.float32)
    return rows[:, 0:tok], rows[:, 128 : 128 + tok] * 256.0 + rows[:, 256 : 256 + tok]


def plane_experts(s_ref, cap_ref, hot_ref, tok):
    base = s_ref[1]
    row = lax.broadcasted_iota(jnp.int32, (DESTS, tok), 0)
    expert = (row // 4) * 16 + (row % 4) * 2 + base
    limit = jnp.zeros((DESTS, tok), jnp.int32)
    for d in range(DESTS):
        e = (d // 4) * 16 + (d % 4) * 2 + base
        cap = jnp.where(e == hot_ref[0], SLOTS, cap_ref[e])
        limit = jnp.where(row == d, cap, limit)
    return expert.astype(jnp.float32), limit.astype(jnp.float32)


def slots_of(named_by, expert, limit, first, tok, turn=0):
    earlier = jnp.where(
        lax.broadcasted_iota(jnp.int32, (tok, tok), 0) < lax.broadcasted_iota(jnp.int32, (tok, tok), 1),
        1.0,
        0.0,
    ).astype(BF)
    named = named_by[0:1, :] == expert
    for k in range(1, TOP):
        named = jnp.logical_or(named, named_by[k : k + 1, :] == expert)
    rank = jnp.dot(jnp.where(named, 1.0, 0.0).astype(BF), earlier, preferred_element_type=jnp.float32)
    kept = jnp.logical_and(named, rank < limit)
    if turn:
        rank = jnp.where(rank < turn, rank + (SLOTS - turn), rank - turn)
    return jnp.where(kept, rank + first, -1.0).astype(jnp.int32)


def match_rows(slots, per, width):
    want = lax.broadcasted_iota(jnp.int32, (DESTS, per, width), 1)
    return want == slots[:, None, :]


def dispatch_kernel(far, s_ref, cap_ref, hot_ref, *refs):
    blocks = 3 if far else 2
    o_ref, factor_refs = refs[blocks], refs[blocks + 1 :]
    refs = refs[:blocks]
    half = 32
    tok = 2 * half
    per = o_ref.shape[1]
    expert, limit = plane_experts(s_ref, cap_ref, hot_ref, tok)
    slots, shares = [], []
    for b, ref in enumerate(refs[:2]):
        routes, weight = read_meta(ref, half, tok)
        turn = EARLY if b == 0 and not far else 0
        slots.append(slots_of(routes, expert, limit, b * SLOTS, tok, turn))
        share = weight / jnp.sum(weight, axis=0, keepdims=True)
        picked = jnp.zeros((DESTS, tok), jnp.float32)
        for k in range(TOP):
            picked = picked + jnp.where(routes[k : k + 1, :] == expert, share[k : k + 1, :], 0.0)
        shares.append(picked)
    slots = jnp.concatenate(slots, axis=1)
    shares = jnp.concatenate(shares, axis=1)
    match = match_rows(slots, per, 2 * tok)
    chosen = jnp.where(match, 1.0, 0.0).reshape(DESTS * per, 2 * tok).astype(BF)
    factor = jnp.where(match, shares[:, None, :], 0.0)
    pieces = [factor[:, LATE:, :], factor[:, 0:LATE, 0:tok]]
    for piece, f_ref in zip(pieces, factor_refs):
        piece = piece.reshape(-1, piece.shape[2]).T
        high = piece.astype(BF)
        f_ref[0] = high
        f_ref[1] = (piece - high.astype(jnp.float32)).astype(BF)
    width = o_ref.shape[2]
    step = 512
    for n in range(0, width, step):
        at = slice(n, n + step)
        rows = []
        for b, ref in enumerate(refs[:2]):
            rows.append(ref[0:half, at])
            if far and b == 1:
                rows.append(refs[2][:, at])
            else:
                rows.append(ref[half + TOP :, at])
        got = jnp.dot(chosen, jnp.concatenate(rows, axis=0), preferred_element_type=jnp.float32)
        o_ref[:, :, at] = got.astype(BF).reshape(DESTS, per, step)


def weighted(f_ref, rows):
    part = jnp.dot(f_ref[0], rows, preferred_element_type=jnp.float32)
    return part + jnp.dot(f_ref[1], rows, preferred_element_type=jnp.float32)


def combine_a_kernel(f_ref, r_ref, one, two_top, two_low):
    half = two_top.shape[0]
    width = r_ref.shape[2]
    step = 512
    for n in range(0, width, step):
        at = slice(n, n + step)
        part = weighted(f_ref, r_ref[:, :, at].reshape(-1, step))
        one[:, at] = part[0 : 2 * half]
        two_top[:, at] = part[2 * half : 3 * half].astype(BF)
        two_low[:, at] = part[3 * half :].astype(BF)


def combine_b_kernel(f_one, f_near, r_ref, one, over_back, over_fwd, own, to_back, to_fwd):
    half = over_back.shape[0]
    width = r_ref.shape[2]
    step = 512
    for n in range(0, width, step):
        at = slice(n, n + step)
        part = one[:, at] + weighted(f_one, r_ref[:, 0:LATE, at].reshape(-1, step))
        to_back[0:half, at] = (part[0:half] + over_back[:, at].astype(jnp.float32)).astype(BF)
        to_back[half:, at] = part[half:].astype(BF)
        part = weighted(f_near, r_ref[:, LATE:, at].reshape(-1, step))
        own[:, at] = part[0 : 2 * half]
        to_fwd[0:half, at] = part[2 * half : 3 * half].astype(BF)
        to_fwd[half:, at] = (part[3 * half :] + over_fwd[:, at].astype(jnp.float32)).astype(BF)


def combine_c_kernel(f_ref, r_ref, own_ref, out_ref):
    width = r_ref.shape[2]
    step = 512
    for n in range(0, width, step):
        at = slice(n, n + step)
        out_ref[:, at] = own_ref[:, at] + weighted(f_ref, r_ref[:, :, at].reshape(-1, step))


def up_kernel(off_ref, xa_ref, xb_ref, *refs):
    groups = refs[0:8]
    tails, heads = (refs[8], refs[10]), (refs[9], refs[11])
    wg, wu, gate_s, sems = refs[12:]
    size = groups[0].shape[1]
    copies = [[], []]
    for which, dst in enumerate((wg, wu)):
        for i in range(8):
            at = pl.multiple_of(off_ref[i] * size, size)
            copies[which].append(
                pltpu.make_async_copy(
                    groups[i].at[which], dst.at[pl.ds(at, size), :], sems.at[which * 8 + i]
                )
            )
    for group in copies:
        for c in group:
            c.start()
    rows = xa_ref.shape[0]
    part = 8
    per = 2 * SLOTS
    step = part * per
    for c in copies[0]:
        c.wait()
    for j, x_ref in enumerate((xa_ref, xb_ref)):
        for r in range(0, rows, step):
            gate_s[j * rows + r : j * rows + r + step, :] = jnp.dot(
                x_ref[r : r + step, :], wg[...], preferred_element_type=jnp.float32
            )
    for c in copies[1]:
        c.wait()
    for j, x_ref in enumerate((xa_ref, xb_ref)):
        for k, r in enumerate(range(0, rows, step)):
            gate = gate_s[j * rows + r : j * rows + r + step, :]
            up = jnp.dot(x_ref[r : r + step, :], wu[...], preferred_element_type=jnp.float32)
            hidden = gate / (1.0 + jnp.exp(-gate)) * up
            hidden = hidden.reshape(part, per, hidden.shape[1])
            tail = part * (per - LATE)
            tails[j][k * tail : (k + 1) * tail, :] = (
                hidden[:, LATE:, :].reshape(tail, hidden.shape[2]).astype(BF)
            )
            head = part * LATE
            heads[j][k * head : (k + 1) * head, :] = (
                hidden[:, 0:LATE, :].reshape(head, hidden.shape[2]).astype(BF)
            )


def down_kernel(count, off_ref, *refs):
    h_refs = refs[0:count]
    downs = refs[count : count + 8]
    o_ref, wd, done, sems, out_sems = refs[count + 8 :]
    size = downs[0].shape[1]
    outs = []
    copies = [pltpu.make_async_copy(downs[i], wd.at[i], sems.at[i]) for i in range(8)]
    for c in copies:
        c.start()
    part = 8
    for i in range(8):
        copies[i].wait()
        at = pl.ds(pl.multiple_of(off_ref[i] * size, size), size)
        first = 0
        for h_ref in h_refs:
            per = h_ref.shape[0] // DESTS
            for d in range(0, DESTS, part):
                got = jnp.dot(
                    h_ref[d * per : (d + part) * per, :], wd[i], preferred_element_type=jnp.float32
                )
                done[i, d : d + part, first : first + per, :] = got.reshape(part, per, size).astype(BF)
            first += per
        outs.append(pltpu.make_async_copy(done.at[i], o_ref.at[:, :, at], out_sems.at[i]))
        outs[i].start()
    for c in outs:
        c.wait()


def cost(flops, moved, hard=0):
    return pl.CostEstimate(flops=flops, bytes_accessed=moved, transcendentals=hard)


def shape(dims, kind=BF):
    return jax.ShapeDtypeStruct(dims, kind)


def exchange(value):
    return lax.all_to_all(value, ("x", "y"), split_axis=0, concat_axis=0, tiled=True)


def per_device(tokens, routes, route_weight, capacity, hot_expert, w_gate, w_up, w_down):
    zp, zq, core, zh = (lax.axis_index(n) for n in ("zp", "zq", "core", "zh"))
    ring = ("zp", "zh")
    order = [0, 2, 1, 3]
    fwd = [(order[i], order[(i + 1) % 4]) for i in range(4)]
    back = [(order[(i + 1) % 4], order[i]) for i in range(4)]
    swap = [(0, 1), (1, 0)]
    tok, width = tokens.shape
    half = tok // 2
    ff = w_gate.shape[2]
    piece = w_gate.shape[1]
    per = 2 * SLOTS
    rows = DESTS * per
    split = half + TOP

    scal = jnp.stack([zp, zh * 8 + zp]).astype(jnp.int32)
    own = pl.pallas_call(
        pack_kernel,
        out_shape=shape((tok + TOP, width)),
        in_specs=[VMEM] * 3,
        out_specs=VMEM,
        compiler_params=grant(56),
        cost_estimate=cost(0, 600 << 10),
        name="pack",
    )(tokens, routes.T, route_weight.T)
    tok3 = lax.ppermute(own, ring, back)
    tok1 = lax.ppermute(own, ring, fwd)
    mine_gu, other_gu, mine_d, other_d = pl.pallas_call(
        weights_kernel,
        out_shape=[shape((2, piece, ff)), shape((2, piece, ff)), shape((ff, piece)), shape((ff, piece))],
        in_specs=[SMEM, ANY, ANY, ANY],
        out_specs=[ANY] * 4,
        scratch_shapes=[
            pltpu.VMEM((2, 2, piece, ff), BF),
            pltpu.VMEM((2, ff, piece), BF),
            pltpu.SemaphoreType.DMA((6,)),
            pltpu.SemaphoreType.DMA((6,)),
        ],
        compiler_params=grant(56),
        cost_estimate=cost(0, 5 << 20),
        name="pack_weights",
    )(scal, w_gate, w_up, w_down)

    def shards(mine, other):
        a = lax.ppermute(other, "zp", swap)
        b = lax.ppermute(mine, "zq", swap)
        c = lax.ppermute(a, "zq", swap)
        near = [lax.ppermute(v, "core", swap) for v in (mine, a, b, c)]
        return [mine, a, b, c] + near

    gates_ups = shards(mine_gu, other_gu)
    downs = shards(mine_d, other_d)

    far_top = lax.ppermute(tok1[:split], ring, fwd)
    far_low = lax.ppermute(tok3[split:], ring, back)

    near = per - LATE

    def dispatch(factor_shapes, *blocks):
        return pl.pallas_call(
            functools.partial(dispatch_kernel, len(blocks) == 3),
            out_shape=[shape((DESTS, per, width))] + [shape((2,) + f) for f in factor_shapes],
            in_specs=[SMEM] * 3 + [VMEM] * len(blocks),
            out_specs=[VMEM] * (1 + len(factor_shapes)),
            compiler_params=grant(12),
            cost_estimate=cost(2 * rows * 2 * tok * width, 2 << 20),
        )(scal, capacity, hot_expert, *blocks)

    split_factors = [(2 * tok, DESTS * near), (tok, DESTS * LATE)]
    sent_b, fac_near, fac_late = dispatch(split_factors, own, tok3)
    x_b = exchange(sent_b).reshape(rows, width)
    sent_a, fac_two, fac_one = dispatch(split_factors, tok1, far_top, far_low)
    x_a = exchange(sent_a).reshape(rows, width)

    place = []
    for g in (0, 1):
        for b in (0, 1):
            for a in (0, 1):
                place.append((zp ^ a) * 4 + (zq ^ b) * 2 + (core ^ g))
    off = jnp.stack(place).astype(jnp.int32)
    h_two, h_one, h_near, h_late = pl.pallas_call(
        up_kernel,
        out_shape=[shape((n, ff)) for n in (DESTS * near, DESTS * LATE) * 2],
        in_specs=[SMEM, VMEM, VMEM] + [ANY] * 8,
        out_specs=[VMEM] * 4,
        scratch_shapes=[pltpu.VMEM((width, ff), BF)] * 2
        + [pltpu.VMEM((2 * rows, ff), jnp.float32), pltpu.SemaphoreType.DMA((16,))],
        compiler_params=grant(GRANT_UP),
        cost_estimate=cost(8 * rows * width * ff, 11 << 20, 2 * rows * ff),
        name="gate_up",
    )(off, x_a, x_b, *gates_ups)

    def down(*hs):
        count = sum(h.shape[0] for h in hs)
        return pl.pallas_call(
            functools.partial(down_kernel, len(hs)),
            out_shape=shape((DESTS, count // DESTS, width)),
            in_specs=[SMEM] + [VMEM] * len(hs) + [ANY] * 8,
            out_specs=ANY,
            scratch_shapes=[
                pltpu.VMEM((8, ff, piece), BF),
                pltpu.VMEM((8, DESTS, count // DESTS, piece), BF),
                pltpu.SemaphoreType.DMA((8,)),
                pltpu.SemaphoreType.DMA((8,)),
            ],
            compiler_params=grant(GRANT_DOWN),
            cost_estimate=cost(2 * count * width * ff, 6 << 20),
        )(off, *hs, *downs)

    def local(kernel, ins, outs, mib):
        return pl.pallas_call(
            kernel,
            out_shape=outs,
            in_specs=[VMEM] * len(ins),
            out_specs=[VMEM] * len(outs),
            compiler_params=grant(mib),
            cost_estimate=cost(1 << 20, 3 << 20),
        )(*ins)

    f32 = jnp.float32
    back_a = exchange(down(h_two))
    back_b = exchange(down(h_one, h_near))
    back_c = exchange(down(h_late))
    block, some, whole = shape((tok, width)), shape((half, width)), shape((tok, width), f32)
    one, two_top, two_low = local(combine_a_kernel, (fac_two, back_a), [whole, some, some], GRANT_A)
    over_back = lax.ppermute(two_top, ring, back)
    over_fwd = lax.ppermute(two_low, ring, fwd)
    part0, to_back, to_fwd = local(
        combine_b_kernel,
        (fac_one, fac_near, back_b, one, over_back, over_fwd),
        [whole, block, block],
        GRANT_B,
    )
    from_next = lax.ppermute(to_back, ring, back)
    from_prev = lax.ppermute(to_fwd, ring, fwd)
    (part0,) = local(combine_c_kernel, (fac_late, back_c, part0), [whole], GRANT_C)
    total = part0 + from_next.astype(f32) + from_prev.astype(f32)
    return total.astype(BF)


def solution(mesh):
    fine = Mesh(mesh.devices.reshape(2, 2, 2, 4, 2, 4), ("zp", "zq", "core", "x", "zh", "y"))
    dp, ex = ("zp", "zq", "core"), ("x", "zh", "y")
    in_specs = (
        P(dp + ex, None),
        P(dp + ex, None),
        P(dp + ex, None),
        P(),
        P(),
        P(ex, dp, None),
        P(ex, dp, None),
        P(ex, None, dp),
    )

    return jax.shard_map(
        per_device, mesh=fine, in_specs=in_specs, out_specs=P(dp + ex, None), check_vma=False
    )
```

profile of v0, /device:TPU:2, one launch (start us, length us, event | category | flops | bytes accessed | tf_op | source)
XLA Modules:
  0.0 251.8 jit_solution(12252892253053678742)
XLA Ops:
  1.7 6.3 %collective-permute-start = (bf16[72,2048]{1,0:T(8,128)(2,1)}, bf16[72,2048]{1,0:T(8,128)(2,1)S(1)}, u32[]{:S(2)}, u32[]{:S(2)}) collective-permute-start(bf16[72,2048]{1,0:T(8,128)(2,1)} %pack.1.refs_0_), channel_id=1, source_target_pairs={{128,0},{4,128},{132,4},{0,132},{129,1},{5,129},{133,5},{1,133},{1... | collective-permute-start | bytes 884744 | tf_op jit(solution)/shard_map/ppermute | solution.py:297
  8.7 12.2 %collective-permute-done.refs_1_ = bf16[72,2048]{1,0:T(8,128)(2,1)S(1)} collective-permute-done((bf16[72,2048]{1,0:T(8,128)(2,1)}, bf16[72,2048]{1,0:T(8,128)(2,1)S(1)}, u32[]{:S(2)}, u32[]{:S(2)}) %collective-permute-start) | collective-permute-done | bytes 294944 | tf_op jit(solution)/shard_map/ppermute | solution.py:297
  22.6 2.5 shard_map.82
  25.1 7.5 %all-to-all-start.1 = ((bf16[16,24,2048]{2,1,0:T(8,128)(2,1)}), bf16[16,24,2048]{2,1,0:T(8,128)(2,1)S(1)}, u32[]{:S(2)}, u32[]{:S(2)}) async-start(bf16[16,24,2048]{2,1,0:T(8,128)(2,1)} %get-tuple-element.27), calls=%async_computation.1 | async-start | bytes 3145728 | tf_op jit(solution)/shard_map/all_to_all | solution.py:269
  32.6 3.3 %pack_weights.1 = (bf16[2,256,768]{2,1,0:T(8,128)(2,1)}, bf16[2,256,768]{2,1,0:T(8,128)(2,1)}, bf16[768,256]{1,0:T(8,128)(2,1)}, bf16[768,256]{1,0:T(8,128)(2,1)}) custom-call(s32[2]{0:T(128)} %copy-done.2, bf16[2,256,768]{2,1,0:T(8,128)(2,1)} %g_ref.1, bf16[2,256,768]{2,1,0:T(8,128)(2,1)} %u_ref.1, bf16[2,768,256]{2,1,0:T(8,128)(2,1)} %d_ref.1), custom_call_target="tpu_custom_call" | custom-call | bytes 5242880 | tf_op jit(solution)/shard_map/pack_weights/pallas_call | solution.py:299
  35.9 2.1 collective-permute-start.4
  38.9 27.7 %collective-permute-done.1.refs_0_ = bf16[72,2048]{1,0:T(8,128)(2,1)S(1)} collective-permute-done((bf16[72,2048]{1,0:T(8,128)(2,1)S(1)}, bf16[72,2048]{1,0:T(8,128)(2,1)S(1)}, u32[]{:S(2)}, u32[]{:S(2)}) %collective-permute-start.1) | collective-permute-done | bytes 294944 | tf_op jit(solution)/shard_map/ppermute | solution.py:298
  66.6 3.5 %collective-permute-start.2 = (bf16[40,2048]{1,0:T(8,128)(2,1)S(1)}, bf16[40,2048]{1,0:T(8,128)(2,1)S(1)}, u32[]{:S(2)}, u32[]{:S(2)}) collective-permute-start(bf16[40,2048]{1,0:T(8,128)(2,1)S(1)} %slice.8), channel_id=1, source_target_pairs={{0,128},{128,4},{4,132},{132,0},{1,129},{129,5},{5,133},{133,1},{2... | collective-permute-start | bytes 491528 | tf_op jit(solution)/shard_map/ppermute | solution.py:325
  70.2 2.6 %collective-permute-start.3 = (bf16[32,2048]{1,0:T(8,128)(2,1)S(1)}, bf16[32,2048]{1,0:T(8,128)(2,1)S(1)}, u32[]{:S(2)}, u32[]{:S(2)}) collective-permute-start(bf16[32,2048]{1,0:T(8,128)(2,1)S(1)} %slice.9), channel_id=1, source_target_pairs={{128,0},{4,128},{132,4},{0,132},{129,1},{5,129},{133,5},{1,133},{1... | collective-permute-start | bytes 393224 | tf_op jit(solution)/shard_map/ppermute | solution.py:326
  72.8 20.3 %collective-permute-start.5 = (bf16[2,256,768]{2,1,0:T(8,128)(2,1)}, bf16[2,256,768]{2,1,0:T(8,128)(2,1)S(1)}, u32[]{:S(2)}, u32[]{:S(2)}) collective-permute-start(bf16[2,256,768]{2,1,0:T(8,128)(2,1)} %get-tuple-element.28.refs_0_), channel_id=1, source_target_pairs={{0,64},{64,0},{1,65},{65,1},{2,66},{66,2},{3,67},{67,3},{4,68},{68... | collective-permute-start | bytes 2359304 | tf_op jit(solution)/shard_map/ppermute | solution.py:317
  93.1 2.6 %shard_map.83 = (bf16[16,24,2048]{2,1,0:T(8,128)(2,1)}, bf16[2,128,256]{2,1,0:T(8,128)(2,1)S(1)}, bf16[2,64,128]{2,1,0:T(8,128)(2,1)S(1)}) custom-call(s32[2]{0:T(128)S(1)} %copy-done.3, s32[64]{0:T(128)S(1)} %copy-done.5, s32[1]{0:T(128)S(6)} %copy.9.hot_ref, bf16[72,2048]{1,0:T(8,128)(2,1)S(1)} %collective-permute-done.1.refs_0_, ...), custom_call_target="tpu_custom_call" | custom-call | flops 201326592 | bytes 2097152 | tf_op jit(solution)/shard_map/pallas_call | solution.py:331
  96.8 7.4 %all-to-all-start = ((bf16[16,24,2048]{2,1,0:T(8,128)(2,1)}), bf16[16,24,2048]{2,1,0:T(8,128)(2,1)}, u32[]{:S(2)}, u32[]{:S(2)}) async-start(bf16[16,24,2048]{2,1,0:T(8,128)(2,1)} %get-tuple-element.26), calls=%async_computation | async-start | bytes 3145728 | tf_op jit(solution)/shard_map/all_to_all | solution.py:269
  104.4 7.9 %collective-permute-start.12 = (bf16[768,256]{1,0:T(8,128)(2,1)S(1)}, bf16[768,256]{1,0:T(8,128)(2,1)S(1)}, u32[]{:S(2)}, u32[]{:S(2)}) collective-permute-start(bf16[768,256]{1,0:T(8,128)(2,1)S(1)} %copy-done.6), channel_id=1, source_target_pairs={{0,64},{64,0},{1,65},{65,1},{2,66},{66,2},{3,67},{67,3},{4,68},{68... | collective-permute-start | bytes 1179656 | tf_op jit(solution)/shard_map/ppermute | solution.py:317
  112.3 10.3 %collective-permute-done.5.refs_2_ = bf16[2,256,768]{2,1,0:T(8,128)(2,1)S(1)} collective-permute-done((bf16[2,256,768]{2,1,0:T(8,128)(2,1)}, bf16[2,256,768]{2,1,0:T(8,128)(2,1)S(1)}, u32[]{:S(2)}, u32[]{:S(2)}) %collective-permute-start.5) | collective-permute-done | bytes 786464 | tf_op jit(solution)/shard_map/ppermute | solution.py:317
  122.7 13.8 %collective-permute-done.11.refs_2_.refs_3_ = bf16[768,256]{1,0:T(8,128)(2,1)S(1)} collective-permute-done((bf16[768,256]{1,0:T(8,128)(2,1)S(1)}, bf16[768,256]{1,0:T(8,128)(2,1)S(1)}, u32[]{:S(2)}, u32[]{:S(2)}) %collective-permute-start.11) | collective-permute-done | bytes 393248 | tf_op jit(solution)/shard_map/ppermute | solution.py:316
  136.5 3.2 %collective-permute-done.6.refs_3_ = bf16[2,256,768]{2,1,0:T(8,128)(2,1)} collective-permute-done((bf16[2,256,768]{2,1,0:T(8,128)(2,1)}, bf16[2,256,768]{2,1,0:T(8,128)(2,1)}, u32[]{:S(2)}, u32[]{:S(2)}) %collective-permute-start.6) | collective-permute-done | bytes 786464 | tf_op jit(solution)/shard_map/ppermute | solution.py:318
  139.6 5.8 %collective-permute-done.12.refs_3_.refs_4_ = bf16[768,256]{1,0:T(8,128)(2,1)S(1)} collective-permute-done((bf16[768,256]{1,0:T(8,128)(2,1)S(1)}, bf16[768,256]{1,0:T(8,128)(2,1)S(1)}, u32[]{:S(2)}, u32[]{:S(2)}) %collective-permute-start.12) | collective-permute-done | bytes 393248 | tf_op jit(solution)/shard_map/ppermute | solution.py:317
  147.0 7.8 %collective-permute-done.13.refs_4_.refs_5_ = bf16[768,256]{1,0:T(8,128)(2,1)S(1)} collective-permute-done((bf16[768,256]{1,0:T(8,128)(2,1)S(1)}, bf16[768,256]{1,0:T(8,128)(2,1)S(1)}, u32[]{:S(2)}, u32[]{:S(2)}) %collective-permute-start.13) | collective-permute-done | bytes 393248 | tf_op jit(solution)/shard_map/ppermute | solution.py:318
  155.5 9.9 %gate_up.1 = (bf16[256,768]{1,0:T(8,128)(2,1)}, bf16[128,768]{1,0:T(8,128)(2,1)}, bf16[256,768]{1,0:T(8,128)(2,1)}, bf16[128,768]{1,0:T(8,128)(2,1)}) custom-call(s32[8]{0:T(128)} %stack.47.off_ref, bf16[384,2048]{1,0:T(8,128)(2,1)} %bitcast.12.xa_ref, bf16[384,2048]{1,0:T(8,128)(2,1)} %bitcast.14, bf16[2,256,768]{2,1,0:T(8,128)(2,1)} %get-tuple-element.28.refs_0_, ...), custom_call_target="tpu_custom_call" | custom-call | flops 4831838208 | bytes 11534336 | tf_op jit(solution)/shard_map/gate_up/pallas_call | solution.py:352
  166.7 5.0 %shard_map.86 = bf16[16,16,2048]{2,1,0:T(8,128)(2,1)} custom-call(s32[8]{0:T(128)} %stack.47.off_ref, bf16[256,768]{1,0:T(8,128)(2,1)} %get-tuple-element.38.refs_0_, bf16[768,256]{1,0:T(8,128)(2,1)} %get-tuple-element.31.refs_1_.refs_2_, bf16[768,256]{1,0:T(8,128)(2,1)} %copy-done.7, bf16[768,256]{1,0:T(8,128)(2,1)} %copy-done.8, ...), custom_call_target="tpu_custom_call" | custom-call | flops 805306368 | bytes 6291456 | tf_op jit(solution)/shard_map/pallas_call | solution.py:366
  171.7 7.2 %all-to-all-start.4 = ((bf16[16,16,2048]{2,1,0:T(8,128)(2,1)}), bf16[16,16,2048]{2,1,0:T(8,128)(2,1)S(1)}, u32[]{:S(2)}, u32[]{:S(2)}) async-start(bf16[16,16,2048]{2,1,0:T(8,128)(2,1)} %shard_map.86), calls=%async_computation.4 | async-start | bytes 2097152 | tf_op jit(solution)/shard_map/all_to_all | solution.py:269
  178.9 6.2 %shard_map.85 = bf16[16,24,2048]{2,1,0:T(8,128)(2,1)} custom-call(s32[8]{0:T(128)} %stack.47.off_ref, bf16[128,768]{1,0:T(8,128)(2,1)} %get-tuple-element.35.refs_0_, bf16[256,768]{1,0:T(8,128)(2,1)} %get-tuple-element.36.refs_1_, bf16[768,256]{1,0:T(8,128)(2,1)} %get-tuple-element.31.refs_1_.refs_2_, bf16[768,256]{1,0:T(8,128)(2,1)} %copy-done.7, ...), custom_call_target="tpu_custom_call" | custom-call | flops 1207959552 | bytes 6291456 | tf_op jit(solution)/shard_map/pallas_call | solution.py:366
  185.2 9.2 %all-to-all-done.4.r_ref = bf16[16,16,2048]{2,1,0:T(8,128)(2,1)S(1)} async-done(((bf16[16,16,2048]{2,1,0:T(8,128)(2,1)}), bf16[16,16,2048]{2,1,0:T(8,128)(2,1)S(1)}, u32[]{:S(2)}, u32[]{:S(2)}) %all-to-all-start.4) | async-done | bytes 1048608 | tf_op jit(solution)/shard_map/all_to_all | solution.py:269
  194.4 6.4 %all-to-all-start.3 = ((bf16[16,24,2048]{2,1,0:T(8,128)(2,1)}), bf16[16,24,2048]{2,1,0:T(8,128)(2,1)S(1)}, u32[]{:S(2)}, u32[]{:S(2)}) async-start(bf16[16,24,2048]{2,1,0:T(8,128)(2,1)} %shard_map.85), calls=%async_computation.3 | async-start | bytes 3145728 | tf_op jit(solution)/shard_map/all_to_all | solution.py:269
  200.7 4.8 %shard_map.84 = bf16[16,8,2048]{2,1,0:T(8,128)(2,1)} custom-call(s32[8]{0:T(128)} %stack.47.off_ref, bf16[128,768]{1,0:T(8,128)(2,1)} %get-tuple-element.30.refs_0_, bf16[768,256]{1,0:T(8,128)(2,1)} %get-tuple-element.31.refs_1_.refs_2_, bf16[768,256]{1,0:T(8,128)(2,1)} %copy-done.7, bf16[768,256]{1,0:T(8,128)(2,1)} %copy-done.8, ...), custom_call_target="tpu_custom_call" | custom-call | flops 402653184 | bytes 6291456 | tf_op jit(solution)/shard_map/pallas_call | solution.py:366
  205.5 15.3 %all-to-all-done.3.r_ref = bf16[16,24,2048]{2,1,0:T(8,128)(2,1)S(1)} async-done(((bf16[16,24,2048]{2,1,0:T(8,128)(2,1)}), bf16[16,24,2048]{2,1,0:T(8,128)(2,1)S(1)}, u32[]{:S(2)}, u32[]{:S(2)}) %all-to-all-start.3) | async-done | bytes 1572896 | tf_op jit(solution)/shard_map/all_to_all | solution.py:269
  220.9 6.0 %all-to-all-start.2 = ((bf16[16,8,2048]{2,1,0:T(8,128)(2,1)}), bf16[16,8,2048]{2,1,0:T(8,128)(2,1)S(1)}, u32[]{:S(2)}, u32[]{:S(2)}) async-start(bf16[16,8,2048]{2,1,0:T(8,128)(2,1)} %shard_map.84), calls=%async_computation.2 | async-start | bytes 1048576 | tf_op jit(solution)/shard_map/all_to_all | solution.py:269
  227.3 2.4 collective-permute-start.18
  230.3 3.9 %collective-permute-done.18.over_back = bf16[32,2048]{1,0:T(8,128)(2,1)S(1)} collective-permute-done((bf16[32,2048]{1,0:T(8,128)(2,1)S(1)}, bf16[32,2048]{1,0:T(8,128)(2,1)S(1)}, u32[]{:S(2)}, u32[]{:S(2)}) %collective-permute-start.18) | collective-permute-done | bytes 131104 | tf_op jit(solution)/shard_map/ppermute | solution.py:397
  234.2 3.9 %collective-permute-done.19.over_fwd = bf16[32,2048]{1,0:T(8,128)(2,1)S(1)} collective-permute-done((bf16[32,2048]{1,0:T(8,128)(2,1)S(1)}, bf16[32,2048]{1,0:T(8,128)(2,1)S(1)}, u32[]{:S(2)}, u32[]{:S(2)}) %collective-permute-start.19) | collective-permute-done | bytes 131104 | tf_op jit(solution)/shard_map/ppermute | solution.py:398
  238.9 2.9 %collective-permute-start.21 = (bf16[64,2048]{1,0:T(8,128)(2,1)S(1)}, bf16[64,2048]{1,0:T(8,128)(2,1)S(1)}, u32[]{:S(2)}, u32[]{:S(2)}) collective-permute-start(bf16[64,2048]{1,0:T(8,128)(2,1)S(1)} %get-tuple-element.44), channel_id=1, source_target_pairs={{0,128},{128,4},{4,132},{132,0},{1,129},{129,5},{5,133},{133,1},{2... | collective-permute-start | bytes 786440 | tf_op jit(solution)/shard_map/ppermute | solution.py:406
  242.1 7.6 %collective-permute-done.20 = bf16[64,2048]{1,0:T(8,128)(2,1)S(1)} collective-permute-done((bf16[64,2048]{1,0:T(8,128)(2,1)S(1)}, bf16[64,2048]{1,0:T(8,128)(2,1)S(1)}, u32[]{:S(2)}, u32[]{:S(2)}) %collective-permute-start.20) | collective-permute-done | bytes 262176 | tf_op jit(solution)/shard_map/ppermute | solution.py:405
  (74 shorter events, 13.3 us)
Async XLA Ops:
  1.7 19.2 %collective-permute-start = (bf16[72,2048]{1,0:T(8,128)(2,1)}, bf16[72,2048]{1,0:T(8,128)(2,1)S(1)}, u32[]{:S(2)}, u32[]{:S(2)}) collective-permute-start(bf16[72,2048]{1,0:T(8,128)(2,1)} %pack.1.refs_0_), channel_id=1, source_target_pairs={{128,0},{4,128},{132,4},{0,132},{129,1},{5,129},{133,5},{1,133},{1... | collective-permute-start | bytes 884744 | tf_op jit(solution)/shard_map/ppermute | solution.py:297
  25.1 70.6 %all-to-all-start.1 = ((bf16[16,24,2048]{2,1,0:T(8,128)(2,1)}), bf16[16,24,2048]{2,1,0:T(8,128)(2,1)S(1)}, u32[]{:S(2)}, u32[]{:S(2)}) async-start(bf16[16,24,2048]{2,1,0:T(8,128)(2,1)} %get-tuple-element.27), calls=%async_computation.1 | async-start | bytes 3145728 | tf_op jit(solution)/shard_map/all_to_all | solution.py:269
  32.5 60.5 %copy-start.3 = (s32[2]{0:T(128)S(1)}, s32[2]{0:T(128)}, u32[]{:S(2)}) copy-start(s32[2]{0:T(128)} %copy-done.2) | copy-start | bytes 28
  32.6 60.5 %copy-start.5 = (s32[64]{0:T(128)S(1)}, s32[64]{0:T(128)}, u32[]{:S(2)}) copy-start(s32[64]{0:T(128)} %cap_ref.3) | copy-start | bytes 772
  35.9 57.1 %collective-permute-start.4 = (bf16[2,256,768]{2,1,0:T(8,128)(2,1)}, bf16[2,256,768]{2,1,0:T(8,128)(2,1)}, u32[]{:S(2)}, u32[]{:S(2)}) collective-permute-start(bf16[2,256,768]{2,1,0:T(8,128)(2,1)} %get-tuple-element.29), channel_id=1, source_target_pairs={{0,128},{128,0},{1,129},{129,1},{2,130},{130,2},{3,131},{131,3},{4... | collective-permute-start | bytes 2359304 | tf_op jit(solution)/shard_map/ppermute | solution.py:316
  38.0 28.6 %collective-permute-start.1 = (bf16[72,2048]{1,0:T(8,128)(2,1)S(1)}, bf16[72,2048]{1,0:T(8,128)(2,1)S(1)}, u32[]{:S(2)}, u32[]{:S(2)}) collective-permute-start(bf16[72,2048]{1,0:T(8,128)(2,1)S(1)} %copy-done.1), channel_id=1, source_target_pairs={{0,128},{128,4},{4,132},{132,0},{1,129},{129,5},{5,133},{133,1},{2... | collective-permute-start | bytes 884744 | tf_op jit(solution)/shard_map/ppermute | solution.py:298
  66.6 26.4 %collective-permute-start.2 = (bf16[40,2048]{1,0:T(8,128)(2,1)S(1)}, bf16[40,2048]{1,0:T(8,128)(2,1)S(1)}, u32[]{:S(2)}, u32[]{:S(2)}) collective-permute-start(bf16[40,2048]{1,0:T(8,128)(2,1)S(1)} %slice.8), channel_id=1, source_target_pairs={{0,128},{128,4},{4,132},{132,0},{1,129},{129,5},{5,133},{133,1},{2... | collective-permute-start | bytes 491528 | tf_op jit(solution)/shard_map/ppermute | solution.py:325
  70.2 22.9 %collective-permute-start.3 = (bf16[32,2048]{1,0:T(8,128)(2,1)S(1)}, bf16[32,2048]{1,0:T(8,128)(2,1)S(1)}, u32[]{:S(2)}, u32[]{:S(2)}) collective-permute-start(bf16[32,2048]{1,0:T(8,128)(2,1)S(1)} %slice.9), channel_id=1, source_target_pairs={{128,0},{4,128},{132,4},{0,132},{129,1},{5,129},{133,5},{1,133},{1... | collective-permute-start | bytes 393224 | tf_op jit(solution)/shard_map/ppermute | solution.py:326
  72.8 49.9 %collective-permute-start.5 = (bf16[2,256,768]{2,1,0:T(8,128)(2,1)}, bf16[2,256,768]{2,1,0:T(8,128)(2,1)S(1)}, u32[]{:S(2)}, u32[]{:S(2)}) collective-permute-start(bf16[2,256,768]{2,1,0:T(8,128)(2,1)} %get-tuple-element.28.refs_0_), channel_id=1, source_target_pairs={{0,64},{64,0},{1,65},{65,1},{2,66},{66,2},{3,67},{67,3},{4,68},{68... | collective-permute-start | bytes 2359304 | tf_op jit(solution)/shard_map/ppermute | solution.py:317
  93.0 46.6 %collective-permute-start.6 = (bf16[2,256,768]{2,1,0:T(8,128)(2,1)}, bf16[2,256,768]{2,1,0:T(8,128)(2,1)}, u32[]{:S(2)}, u32[]{:S(2)}) collective-permute-start(bf16[2,256,768]{2,1,0:T(8,128)(2,1)} %collective-permute-done.4.refs_1_), channel_id=1, source_target_pairs={{0,64},{64,0},{1,65},{65,1},{2,66},{66,2},{3,67},{67,3},{4,68},{68... | collective-permute-start | bytes 2359304 | tf_op jit(solution)/shard_map/ppermute | solution.py:318
  96.8 58.7 %all-to-all-start = ((bf16[16,24,2048]{2,1,0:T(8,128)(2,1)}), bf16[16,24,2048]{2,1,0:T(8,128)(2,1)}, u32[]{:S(2)}, u32[]{:S(2)}) async-start(bf16[16,24,2048]{2,1,0:T(8,128)(2,1)} %get-tuple-element.26), calls=%async_computation | async-start | bytes 3145728 | tf_op jit(solution)/shard_map/all_to_all | solution.py:269
  104.2 32.3 %collective-permute-start.11 = (bf16[768,256]{1,0:T(8,128)(2,1)S(1)}, bf16[768,256]{1,0:T(8,128)(2,1)S(1)}, u32[]{:S(2)}, u32[]{:S(2)}) collective-permute-start(bf16[768,256]{1,0:T(8,128)(2,1)S(1)} %copy-done.17), channel_id=1, source_target_pairs={{0,128},{128,0},{1,129},{129,1},{2,130},{130,2},{3,131},{131,3},{4... | collective-permute-start | bytes 1179656 | tf_op jit(solution)/shard_map/ppermute | solution.py:316
  104.3 42.7 %collective-permute-start.7 = (bf16[2,256,768]{2,1,0:T(8,128)(2,1)S(1)}, bf16[2,256,768]{2,1,0:T(8,128)(2,1)}, u32[]{:S(2)}, u32[]{:S(2)}) collective-permute-start(bf16[2,256,768]{2,1,0:T(8,128)(2,1)S(1)} %copy-done.15), channel_id=1, source_target_pairs={{0,32},{32,0},{1,33},{33,1},{2,34},{34,2},{3,35},{35,3},{4,36},{36... | collective-permute-start | bytes 2359304 | tf_op jit(solution)/shard_map/ppermute | solution.py:319
  104.4 41.0 %collective-permute-start.12 = (bf16[768,256]{1,0:T(8,128)(2,1)S(1)}, bf16[768,256]{1,0:T(8,128)(2,1)S(1)}, u32[]{:S(2)}, u32[]{:S(2)}) collective-permute-start(bf16[768,256]{1,0:T(8,128)(2,1)S(1)} %copy-done.6), channel_id=1, source_target_pairs={{0,64},{64,0},{1,65},{65,1},{2,66},{66,2},{3,67},{67,3},{4,68},{68... | collective-permute-start | bytes 1179656 | tf_op jit(solution)/shard_map/ppermute | solution.py:317
  122.7 32.1 %copy-start.16 = (bf16[2,256,768]{2,1,0:T(8,128)(2,1)}, bf16[2,256,768]{2,1,0:T(8,128)(2,1)S(1)}, u32[]{:S(2)}) copy-start(bf16[2,256,768]{2,1,0:T(8,128)(2,1)S(1)} %collective-permute-done.5.refs_2_) | copy-start | bytes 2359300
  122.7 32.1 %collective-permute-start.9 = (bf16[2,256,768]{2,1,0:T(8,128)(2,1)S(1)}, bf16[2,256,768]{2,1,0:T(8,128)(2,1)}, u32[]{:S(2)}, u32[]{:S(2)}) collective-permute-start(bf16[2,256,768]{2,1,0:T(8,128)(2,1)S(1)} %collective-permute-done.5.refs_2_), channel_id=1, source_target_pairs={{0,32},{32,0},{1,33},{33,1},{2,34},{34,2},{3,35},{35,3},{4,36},{36... | collective-permute-start | bytes 2359304 | tf_op jit(solution)/shard_map/ppermute | solution.py:319
  136.5 29.0 %copy-start.7 = (bf16[768,256]{1,0:T(8,128)(2,1)}, bf16[768,256]{1,0:T(8,128)(2,1)S(1)}, u32[]{:S(2)}) copy-start(bf16[768,256]{1,0:T(8,128)(2,1)S(1)} %collective-permute-done.11.refs_2_.refs_3_) | copy-start | bytes 1179652
  136.5 18.8 %collective-permute-start.8 = (bf16[2,256,768]{2,1,0:T(8,128)(2,1)}, bf16[2,256,768]{2,1,0:T(8,128)(2,1)}, u32[]{:S(2)}, u32[]{:S(2)}) collective-permute-start(bf16[2,256,768]{2,1,0:T(8,128)(2,1)} %collective-permute-done.4.refs_1_), channel_id=1, source_target_pairs={{0,32},{32,0},{1,33},{33,1},{2,34},{34,2},{3,35},{35,3},{4,36},{36... | collective-permute-start | bytes 2359304 | tf_op jit(solution)/shard_map/ppermute | solution.py:319
  139.6 15.9 %collective-permute-start.10 = (bf16[2,256,768]{2,1,0:T(8,128)(2,1)}, bf16[2,256,768]{2,1,0:T(8,128)(2,1)}, u32[]{:S(2)}, u32[]{:S(2)}) collective-permute-start(bf16[2,256,768]{2,1,0:T(8,128)(2,1)} %collective-permute-done.6.refs_3_), channel_id=1, source_target_pairs={{0,32},{32,0},{1,33},{33,1},{2,34},{34,2},{3,35},{35,3},{4,36},{36... | collective-permute-start | bytes 2359304 | tf_op jit(solution)/shard_map/ppermute | solution.py:319
  145.5 20.0 %copy-start.8 = (bf16[768,256]{1,0:T(8,128)(2,1)}, bf16[768,256]{1,0:T(8,128)(2,1)S(1)}, u32[]{:S(2)}) copy-start(bf16[768,256]{1,0:T(8,128)(2,1)S(1)} %collective-permute-done.12.refs_3_.refs_4_) | copy-start | bytes 1179652
  145.5 9.3 %collective-permute-start.13 = (bf16[768,256]{1,0:T(8,128)(2,1)S(1)}, bf16[768,256]{1,0:T(8,128)(2,1)S(1)}, u32[]{:S(2)}, u32[]{:S(2)}) collective-permute-start(bf16[768,256]{1,0:T(8,128)(2,1)S(1)} %collective-permute-done.11.refs_2_.refs_3_), channel_id=1, source_target_pairs={{0,64},{64,0},{1,65},{65,1},{2,66},{66,2},{3,67},{67,3},{4,68},{68... | collective-permute-start | bytes 1179656 | tf_op jit(solution)/shard_map/ppermute | solution.py:318
  147.0 18.5 %collective-permute-start.14 = (bf16[768,256]{1,0:T(8,128)(2,1)S(1)}, bf16[768,256]{1,0:T(8,128)(2,1)S(1)}, u32[]{:S(2)}, u32[]{:S(2)}) collective-permute-start(bf16[768,256]{1,0:T(8,128)(2,1)S(1)} %copy-done.6), channel_id=1, source_target_pairs={{0,32},{32,0},{1,33},{33,1},{2,34},{34,2},{3,35},{35,3},{4,36},{36... | collective-permute-start | bytes 1179656 | tf_op jit(solution)/shard_map/ppermute | solution.py:319
  154.7 10.8 %collective-permute-start.15 = (bf16[768,256]{1,0:T(8,128)(2,1)S(1)}, bf16[768,256]{1,0:T(8,128)(2,1)S(1)}, u32[]{:S(2)}, u32[]{:S(2)}) collective-permute-start(bf16[768,256]{1,0:T(8,128)(2,1)S(1)} %collective-permute-done.11.refs_2_.refs_3_), channel_id=1, source_target_pairs={{0,32},{32,0},{1,33},{33,1},{2,34},{34,2},{3,35},{35,3},{4,36},{36... | collective-permute-start | bytes 1179656 | tf_op jit(solution)/shard_map/ppermute | solution.py:319
  154.8 10.8 %collective-permute-start.16 = (bf16[768,256]{1,0:T(8,128)(2,1)S(1)}, bf16[768,256]{1,0:T(8,128)(2,1)S(1)}, u32[]{:S(2)}, u32[]{:S(2)}) collective-permute-start(bf16[768,256]{1,0:T(8,128)(2,1)S(1)} %collective-permute-done.12.refs_3_.refs_4_), channel_id=1, source_target_pairs={{0,32},{32,0},{1,33},{33,1},{2,34},{34,2},{3,35},{35,3},{4,36},{36... | collective-permute-start | bytes 1179656 | tf_op jit(solution)/shard_map/ppermute | solution.py:319
  155.3 10.3 %collective-permute-start.17 = (bf16[768,256]{1,0:T(8,128)(2,1)S(1)}, bf16[768,256]{1,0:T(8,128)(2,1)S(1)}, u32[]{:S(2)}, u32[]{:S(2)}) collective-permute-start(bf16[768,256]{1,0:T(8,128)(2,1)S(1)} %collective-permute-done.13.refs_4_.refs_5_), channel_id=1, source_target_pairs={{0,32},{32,0},{1,33},{33,1},{2,34},{34,2},{3,35},{35,3},{4,36},{36... | collective-permute-start | bytes 1179656 | tf_op jit(solution)/shard_map/ppermute | solution.py:319
  171.7 22.7 %all-to-all-start.4 = ((bf16[16,16,2048]{2,1,0:T(8,128)(2,1)}), bf16[16,16,2048]{2,1,0:T(8,128)(2,1)S(1)}, u32[]{:S(2)}, u32[]{:S(2)}) async-start(bf16[16,16,2048]{2,1,0:T(8,128)(2,1)} %shard_map.86), calls=%async_computation.4 | async-start | bytes 2097152 | tf_op jit(solution)/shard_map/all_to_all | solution.py:269
  194.4 26.5 %all-to-all-start.3 = ((bf16[16,24,2048]{2,1,0:T(8,128)(2,1)}), bf16[16,24,2048]{2,1,0:T(8,128)(2,1)S(1)}, u32[]{:S(2)}, u32[]{:S(2)}) async-start(bf16[16,24,2048]{2,1,0:T(8,128)(2,1)} %shard_map.85), calls=%async_computation.3 | async-start | bytes 3145728 | tf_op jit(solution)/shard_map/all_to_all | solution.py:269
  220.9 20.9 %all-to-all-start.2 = ((bf16[16,8,2048]{2,1,0:T(8,128)(2,1)}), bf16[16,8,2048]{2,1,0:T(8,128)(2,1)S(1)}, u32[]{:S(2)}, u32[]{:S(2)}) async-start(bf16[16,8,2048]{2,1,0:T(8,128)(2,1)} %shard_map.84), calls=%async_computation.2 | async-start | bytes 1048576 | tf_op jit(solution)/shard_map/all_to_all | solution.py:269
  227.3 6.9 %collective-permute-start.18 = (bf16[32,2048]{1,0:T(8,128)(2,1)S(1)}, bf16[32,2048]{1,0:T(8,128)(2,1)S(1)}, u32[]{:S(2)}, u32[]{:S(2)}) collective-permute-start(bf16[32,2048]{1,0:T(8,128)(2,1)S(1)} %get-tuple-element.40), channel_id=1, source_target_pairs={{128,0},{4,128},{132,4},{0,132},{129,1},{5,129},{133,5},{1,133},{1... | collective-permute-start | bytes 393224 | tf_op jit(solution)/shard_map/ppermute | solution.py:397
  229.7 8.4 %collective-permute-start.19 = (bf16[32,2048]{1,0:T(8,128)(2,1)S(1)}, bf16[32,2048]{1,0:T(8,128)(2,1)S(1)}, u32[]{:S(2)}, u32[]{:S(2)}) collective-permute-start(bf16[32,2048]{1,0:T(8,128)(2,1)S(1)} %get-tuple-element.41), channel_id=1, source_target_pairs={{0,128},{128,4},{4,132},{132,0},{1,129},{129,5},{5,133},{133,1},{2... | collective-permute-start | bytes 393224 | tf_op jit(solution)/shard_map/ppermute | solution.py:398
  238.8 10.9 %collective-permute-start.20 = (bf16[64,2048]{1,0:T(8,128)(2,1)S(1)}, bf16[64,2048]{1,0:T(8,128)(2,1)S(1)}, u32[]{:S(2)}, u32[]{:S(2)}) collective-permute-start(bf16[64,2048]{1,0:T(8,128)(2,1)S(1)} %get-tuple-element.43), channel_id=1, source_target_pairs={{128,0},{4,128},{132,4},{0,132},{129,1},{5,129},{133,5},{1,133},{1... | collective-permute-start | bytes 786440 | tf_op jit(solution)/shard_map/ppermute | solution.py:405
  238.9 12.1 %collective-permute-start.21 = (bf16[64,2048]{1,0:T(8,128)(2,1)S(1)}, bf16[64,2048]{1,0:T(8,128)(2,1)S(1)}, u32[]{:S(2)}, u32[]{:S(2)}) collective-permute-start(bf16[64,2048]{1,0:T(8,128)(2,1)S(1)} %get-tuple-element.44), channel_id=1, source_target_pairs={{0,128},{128,4},{4,132},{132,0},{1,129},{129,5},{5,133},{133,1},{2... | collective-permute-start | bytes 786440 | tf_op jit(solution)/shard_map/ppermute | solution.py:406
  (13 other events, 61.5 us)
where the time goes:
time: 252 us
  waiting for transfers between devices  122 us (48%)
  starting transfers between devices  85.9 us (34%)
  Pallas kernels  37.5 us (15%)
  local copies, waits for them, and re-layouts  4.53 us (2%)
    all_to_all x5, starting transfers between devices, exchange(): lax.all_to_all(value, ('x', 'y'), split_axis=0, concat_axis=0, tiled=True)  34.4 us
    ppermute x2, starting transfers between devices, shards(): b = lax.ppermute(mine, 'zq', swap)  28.2 us
    ppermute x1, waiting for transfers between devices, per_device(): tok1 = lax.ppermute(own, ring, fwd)  27.7 us
    all_to_all x5, waiting for transfers between devices, exchange(): lax.all_to_all(value, ('x', 'y'), split_axis=0, concat_axis=0, tiled=True)  24.6 us
    ppermute x2, waiting for transfers between devices, shards(): b = lax.ppermute(mine, 'zq', swap)  16.1 us
    pallas_call x3, Pallas kernels, down(): pl.pallas_call(functools.partial(down_kernel, len(hs)), out_shape=shape((...  16 us
    ppermute x2, waiting for transfers between devices, shards(): a = lax.ppermute(other, 'zp', swap)  13.8 us
    ppermute x1, waiting for transfers between devices, per_device(): tok3 = lax.ppermute(own, ring, back)  12.2 us
  transfers between devices with their start and end apart: 27, of which 13 were waited for; matrix products, arithmetic and copies ran while one was open for 0% of the time, Pallas kernels for 11%

commit v1 on v0

--- a/solution.py
+++ b/solution.py
@@ -232,18 +232,25 @@
 def down_kernel(count, off_ref, *refs):
     h_refs = refs[0:count]
     downs = refs[count : count + 8]
-    o_ref, wd, done, sems, out_sems = refs[count + 8 :]
+    o_ref, wd, done, sems, out_sems = refs[count + 8 : count + 13]
+    kept = refs[count + 13 : 2 * count + 13]
+    row_sems = refs[2 * count + 13]
     size = downs[0].shape[1]
     outs = []
+    rows = [pltpu.make_async_copy(h_refs[j], kept[j], row_sems.at[j]) for j in range(count)]
+    for c in rows:
+        c.start()
     copies = [pltpu.make_async_copy(downs[i], wd.at[i], sems.at[i]) for i in range(8)]
     for c in copies:
         c.start()
+    for c in rows:
+        c.wait()
     part = 8
     for i in range(8):
         copies[i].wait()
         at = pl.ds(pl.multiple_of(off_ref[i] * size, size), size)
         first = 0
-        for h_ref in h_refs:
+        for h_ref in kept:
             per = h_ref.shape[0] // DESTS
             for d in range(0, DESTS, part):
                 got = jnp.dot(
@@ -333,7 +340,7 @@
             out_shape=[shape((DESTS, per, width))] + [shape((2,) + f) for f in factor_shapes],
             in_specs=[SMEM] * 3 + [VMEM] * len(blocks),
             out_specs=[VMEM] * (1 + len(factor_shapes)),
-            compiler_params=grant(12),
+            compiler_params=grant(54 if len(blocks) == 3 else 12),
             cost_estimate=cost(2 * rows * 2 * tok * width, 2 << 20),
         )(scal, capacity, hot_expert, *blocks)
 
@@ -366,14 +373,16 @@
         return pl.pallas_call(
             functools.partial(down_kernel, len(hs)),
             out_shape=shape((DESTS, count // DESTS, width)),
-            in_specs=[SMEM] + [VMEM] * len(hs) + [ANY] * 8,
+            in_specs=[SMEM] + [ANY] * len(hs) + [ANY] * 8,
             out_specs=ANY,
             scratch_shapes=[
                 pltpu.VMEM((8, ff, piece), BF),
                 pltpu.VMEM((8, DESTS, count // DESTS, piece), BF),
                 pltpu.SemaphoreType.DMA((8,)),
                 pltpu.SemaphoreType.DMA((8,)),
-            ],
+            ]
+            + [pltpu.VMEM(h.shape, BF) for h in hs]
+            + [pltpu.SemaphoreType.DMA((len(hs),))],
             compiler_params=grant(GRANT_DOWN),
             cost_estimate=cost(2 * count * width * ff, 6 << 20),
         )(off, *hs, *downs)

time: 252 us -> 253 us (level)
  waiting for transfers between devices: 122 us -> 119 us
    unnamed x36 -> x42, local copies, waits for them, and re-layouts: 3.9 us -> 5.33 us
  transfers between devices with their start and end apart: 27 -> 27, of which waited for: 13 -> 13; matrix products, arithmetic and copies ran while one was open for 0% -> 0% of each run, Pallas kernels for 11% -> 12%
where the time goes in v1:
time: 253 us; the launch traced here: 252 us
  waiting for transfers between devices  119 us (47%)
  starting transfers between devices  85.9 us (34%)
  Pallas kernels  39.5 us (16%)
  local copies, waits for them, and re-layouts  5.97 us (2%)
    all_to_all x5, starting transfers between devices, exchange(): lax.all_to_all(value, ('x', 'y'), split_axis=0, concat_axis=0, tiled=True)  34.4 us
    ppermute x2, starting transfers between devices, shards(): b = lax.ppermute(mine, 'zq', swap)  28.2 us
    ppermute x1, waiting for transfers between devices, per_device(): tok1 = lax.ppermute(own, ring, fwd)  27.7 us
    all_to_all x5, waiting for transfers between devices, exchange(): lax.all_to_all(value, ('x', 'y'), split_axis=0, concat_axis=0, tiled=True)  23.5 us
    pallas_call x3, Pallas kernels, down(): pl.pallas_call(functools.partial(down_kernel, len(hs)), out_shape=shape((...  17.6 us
    ppermute x2, waiting for transfers between devices, shards(): b = lax.ppermute(mine, 'zq', swap)  14.3 us
    ppermute x2, waiting for transfers between devices, shards(): a = lax.ppermute(other, 'zp', swap)  13.8 us
    ppermute x1, waiting for transfers between devices, per_device(): tok3 = lax.ppermute(own, ring, back)  12.2 us
  transfers between devices with their start and end apart: 27, of which 13 were waited for; matrix products, arithmetic and copies ran while one was open for 0% of the time, Pallas kernels for 12%

profile of v1, /device:TPU:2, one launch (start us, length us, event | category | flops | bytes accessed | tf_op | source)
XLA Modules:
  0.0 252.3 jit_solution(7035282721983165279)
XLA Ops:
  1.7 6.3 %collective-permute-start = (bf16[72,2048]{1,0:T(8,128)(2,1)}, bf16[72,2048]{1,0:T(8,128)(2,1)S(1)}, u32[]{:S(2)}, u32[]{:S(2)}) collective-permute-start(bf16[72,2048]{1,0:T(8,128)(2,1)} %pack.1.refs_0_), channel_id=1, source_target_pairs={{128,0},{4,128},{132,4},{0,132},{129,1},{5,129},{133,5},{1,133},{1... | collective-permute-start | bytes 884744 | tf_op jit(solution)/shard_map/ppermute | solution.py:304
  8.7 12.2 %collective-permute-done.refs_1_ = bf16[72,2048]{1,0:T(8,128)(2,1)S(1)} collective-permute-done((bf16[72,2048]{1,0:T(8,128)(2,1)}, bf16[72,2048]{1,0:T(8,128)(2,1)S(1)}, u32[]{:S(2)}, u32[]{:S(2)}) %collective-permute-start) | collective-permute-done | bytes 294944 | tf_op jit(solution)/shard_map/ppermute | solution.py:304
  22.6 2.5 shard_map.82
  25.0 7.5 %all-to-all-start.1 = ((bf16[16,24,2048]{2,1,0:T(8,128)(2,1)}), bf16[16,24,2048]{2,1,0:T(8,128)(2,1)S(1)}, u32[]{:S(2)}, u32[]{:S(2)}) async-start(bf16[16,24,2048]{2,1,0:T(8,128)(2,1)} %get-tuple-element.27), calls=%async_computation.1 | async-start | bytes 3145728 | tf_op jit(solution)/shard_map/all_to_all | solution.py:276
  32.5 3.4 %pack_weights.1 = (bf16[2,256,768]{2,1,0:T(8,128)(2,1)}, bf16[2,256,768]{2,1,0:T(8,128)(2,1)}, bf16[768,256]{1,0:T(8,128)(2,1)}, bf16[768,256]{1,0:T(8,128)(2,1)}) custom-call(s32[2]{0:T(128)} %copy-done.4, bf16[2,256,768]{2,1,0:T(8,128)(2,1)} %g_ref.1, bf16[2,256,768]{2,1,0:T(8,128)(2,1)} %u_ref.1, bf16[2,768,256]{2,1,0:T(8,128)(2,1)} %d_ref.1), custom_call_target="tpu_custom_call" | custom-call | bytes 5242880 | tf_op jit(solution)/shard_map/pack_weights/pallas_call | solution.py:306
  35.9 2.1 collective-permute-start.4
  38.9 27.7 %collective-permute-done.1.refs_0_ = bf16[72,2048]{1,0:T(8,128)(2,1)S(1)} collective-permute-done((bf16[72,2048]{1,0:T(8,128)(2,1)S(1)}, bf16[72,2048]{1,0:T(8,128)(2,1)S(1)}, u32[]{:S(2)}, u32[]{:S(2)}) %collective-permute-start.1) | collective-permute-done | bytes 294944 | tf_op jit(solution)/shard_map/ppermute | solution.py:305
  66.6 3.5 %collective-permute-start.2 = (bf16[40,2048]{1,0:T(8,128)(2,1)S(1)}, bf16[40,2048]{1,0:T(8,128)(2,1)S(1)}, u32[]{:S(2)}, u32[]{:S(2)}) collective-permute-start(bf16[40,2048]{1,0:T(8,128)(2,1)S(1)} %slice.8), channel_id=1, source_target_pairs={{0,128},{128,4},{4,132},{132,0},{1,129},{129,5},{5,133},{133,1},{2... | collective-permute-start | bytes 491528 | tf_op jit(solution)/shard_map/ppermute | solution.py:332
  70.2 2.6 %collective-permute-start.3 = (bf16[32,2048]{1,0:T(8,128)(2,1)S(1)}, bf16[32,2048]{1,0:T(8,128)(2,1)S(1)}, u32[]{:S(2)}, u32[]{:S(2)}) collective-permute-start(bf16[32,2048]{1,0:T(8,128)(2,1)S(1)} %slice.9), channel_id=1, source_target_pairs={{128,0},{4,128},{132,4},{0,132},{129,1},{5,129},{133,5},{1,133},{1... | collective-permute-start | bytes 393224 | tf_op jit(solution)/shard_map/ppermute | solution.py:333
  72.7 20.3 %collective-permute-start.5 = (bf16[2,256,768]{2,1,0:T(8,128)(2,1)}, bf16[2,256,768]{2,1,0:T(8,128)(2,1)S(1)}, u32[]{:S(2)}, u32[]{:S(2)}) collective-permute-start(bf16[2,256,768]{2,1,0:T(8,128)(2,1)} %get-tuple-element.28.refs_0_), channel_id=1, source_target_pairs={{0,64},{64,0},{1,65},{65,1},{2,66},{66,2},{3,67},{67,3},{4,68},{68... | collective-permute-start | bytes 2359304 | tf_op jit(solution)/shard_map/ppermute | solution.py:324
  94.4 3.0 %shard_map.83 = (bf16[16,24,2048]{2,1,0:T(8,128)(2,1)}, bf16[2,128,256]{2,1,0:T(8,128)(2,1)}, bf16[2,64,128]{2,1,0:T(8,128)(2,1)}) custom-call(s32[2]{0:T(128)} %copy-done.4, s32[64]{0:T(128)} %cap_ref.3, s32[1]{0:T(128)S(6)} %copy.9.hot_ref, bf16[72,2048]{1,0:T(8,128)(2,1)} %copy-done.15, bf16[40,2048]{1,0:T(8,128)(2,1)} %copy-done.19, ...), custom_call_target="tpu_custom_call" | custom-call | flops 201326592 | bytes 2097152 | tf_op jit(solution)/shard_map/pallas_call | solution.py:338
  98.6 7.4 %all-to-all-start = ((bf16[16,24,2048]{2,1,0:T(8,128)(2,1)}), bf16[16,24,2048]{2,1,0:T(8,128)(2,1)}, u32[]{:S(2)}, u32[]{:S(2)}) async-start(bf16[16,24,2048]{2,1,0:T(8,128)(2,1)} %get-tuple-element.26), calls=%async_computation | async-start | bytes 3145728 | tf_op jit(solution)/shard_map/all_to_all | solution.py:276
  106.2 7.9 %collective-permute-start.12 = (bf16[768,256]{1,0:T(8,128)(2,1)S(1)}, bf16[768,256]{1,0:T(8,128)(2,1)S(1)}, u32[]{:S(2)}, u32[]{:S(2)}) collective-permute-start(bf16[768,256]{1,0:T(8,128)(2,1)S(1)} %copy-done.6), channel_id=1, source_target_pairs={{0,64},{64,0},{1,65},{65,1},{2,66},{66,2},{3,67},{67,3},{4,68},{68... | collective-permute-start | bytes 1179656 | tf_op jit(solution)/shard_map/ppermute | solution.py:324
  114.1 8.5 %collective-permute-done.5.refs_2_ = bf16[2,256,768]{2,1,0:T(8,128)(2,1)S(1)} collective-permute-done((bf16[2,256,768]{2,1,0:T(8,128)(2,1)}, bf16[2,256,768]{2,1,0:T(8,128)(2,1)S(1)}, u32[]{:S(2)}, u32[]{:S(2)}) %collective-permute-start.5) | collective-permute-done | bytes 786464 | tf_op jit(solution)/shard_map/ppermute | solution.py:324
  122.7 13.8 %collective-permute-done.11.refs_2_.refs_3_ = bf16[768,256]{1,0:T(8,128)(2,1)S(1)} collective-permute-done((bf16[768,256]{1,0:T(8,128)(2,1)S(1)}, bf16[768,256]{1,0:T(8,128)(2,1)S(1)}, u32[]{:S(2)}, u32[]{:S(2)}) %collective-permute-start.11) | collective-permute-done | bytes 393248 | tf_op jit(solution)/shard_map/ppermute | solution.py:323
  136.5 3.2 %collective-permute-done.6.refs_3_ = bf16[2,256,768]{2,1,0:T(8,128)(2,1)} collective-permute-done((bf16[2,256,768]{2,1,0:T(8,128)(2,1)}, bf16[2,256,768]{2,1,0:T(8,128)(2,1)}, u32[]{:S(2)}, u32[]{:S(2)}) %collective-permute-start.6) | collective-permute-done | bytes 786464 | tf_op jit(solution)/shard_map/ppermute | solution.py:325
  139.6 5.8 %collective-permute-done.12.refs_3_.refs_4_ = bf16[768,256]{1,0:T(8,128)(2,1)S(1)} collective-permute-done((bf16[768,256]{1,0:T(8,128)(2,1)S(1)}, bf16[768,256]{1,0:T(8,128)(2,1)S(1)}, u32[]{:S(2)}, u32[]{:S(2)}) %collective-permute-start.12) | collective-permute-done | bytes 393248 | tf_op jit(solution)/shard_map/ppermute | solution.py:324
  147.0 7.7 %collective-permute-done.13.refs_4_.refs_5_ = bf16[768,256]{1,0:T(8,128)(2,1)S(1)} collective-permute-done((bf16[768,256]{1,0:T(8,128)(2,1)S(1)}, bf16[768,256]{1,0:T(8,128)(2,1)S(1)}, u32[]{:S(2)}, u32[]{:S(2)}) %collective-permute-start.13) | collective-permute-done | bytes 393248 | tf_op jit(solution)/shard_map/ppermute | solution.py:325
  155.5 9.9 %gate_up.1 = (bf16[256,768]{1,0:T(8,128)(2,1)}, bf16[128,768]{1,0:T(8,128)(2,1)}, bf16[256,768]{1,0:T(8,128)(2,1)}, bf16[128,768]{1,0:T(8,128)(2,1)}) custom-call(s32[8]{0:T(128)} %stack.47.off_ref, bf16[384,2048]{1,0:T(8,128)(2,1)} %bitcast.12.xa_ref, bf16[384,2048]{1,0:T(8,128)(2,1)} %bitcast.14, bf16[2,256,768]{2,1,0:T(8,128)(2,1)} %get-tuple-element.28.refs_0_, ...), custom_call_target="tpu_custom_call" | custom-call | flops 4831838208 | bytes 11534336 | tf_op jit(solution)/shard_map/gate_up/pallas_call | solution.py:359
  166.7 5.5 %shard_map.86 = bf16[16,16,2048]{2,1,0:T(8,128)(2,1)} custom-call(s32[8]{0:T(128)} %stack.47.off_ref, bf16[256,768]{1,0:T(8,128)(2,1)} %get-tuple-element.38.refs_0_, bf16[768,256]{1,0:T(8,128)(2,1)} %get-tuple-element.31.refs_1_.refs_2_, bf16[768,256]{1,0:T(8,128)(2,1)} %copy-done.7, bf16[768,256]{1,0:T(8,128)(2,1)} %copy-done.8, ...), custom_call_target="tpu_custom_call" | custom-call | flops 805306368 | bytes 6291456 | tf_op jit(solution)/shard_map/pallas_call | solution.py:373
  172.2 7.2 %all-to-all-start.4 = ((bf16[16,16,2048]{2,1,0:T(8,128)(2,1)}), bf16[16,16,2048]{2,1,0:T(8,128)(2,1)S(1)}, u32[]{:S(2)}, u32[]{:S(2)}) async-start(bf16[16,16,2048]{2,1,0:T(8,128)(2,1)} %shard_map.86), calls=%async_computation.4 | async-start | bytes 2097152 | tf_op jit(solution)/shard_map/all_to_all | solution.py:276
  179.5 6.7 %shard_map.85 = bf16[16,24,2048]{2,1,0:T(8,128)(2,1)} custom-call(s32[8]{0:T(128)} %stack.47.off_ref, bf16[128,768]{1,0:T(8,128)(2,1)} %get-tuple-element.35.refs_0_, bf16[256,768]{1,0:T(8,128)(2,1)} %get-tuple-element.36.refs_1_, bf16[768,256]{1,0:T(8,128)(2,1)} %get-tuple-element.31.refs_1_.refs_2_, bf16[768,256]{1,0:T(8,128)(2,1)} %copy-done.7, ...), custom_call_target="tpu_custom_call" | custom-call | flops 1207959552 | bytes 6291456 | tf_op jit(solution)/shard_map/pallas_call | solution.py:373
  186.1 8.8 %all-to-all-done.4.r_ref = bf16[16,16,2048]{2,1,0:T(8,128)(2,1)S(1)} async-done(((bf16[16,16,2048]{2,1,0:T(8,128)(2,1)}), bf16[16,16,2048]{2,1,0:T(8,128)(2,1)S(1)}, u32[]{:S(2)}, u32[]{:S(2)}) %all-to-all-start.4) | async-done | bytes 1048608 | tf_op jit(solution)/shard_map/all_to_all | solution.py:276
  194.9 6.4 %all-to-all-start.3 = ((bf16[16,24,2048]{2,1,0:T(8,128)(2,1)}), bf16[16,24,2048]{2,1,0:T(8,128)(2,1)S(1)}, u32[]{:S(2)}, u32[]{:S(2)}) async-start(bf16[16,24,2048]{2,1,0:T(8,128)(2,1)} %shard_map.85), calls=%async_computation.3 | async-start | bytes 3145728 | tf_op jit(solution)/shard_map/all_to_all | solution.py:276
  201.3 5.4 %shard_map.84 = bf16[16,8,2048]{2,1,0:T(8,128)(2,1)} custom-call(s32[8]{0:T(128)} %stack.47.off_ref, bf16[128,768]{1,0:T(8,128)(2,1)} %get-tuple-element.30.refs_0_, bf16[768,256]{1,0:T(8,128)(2,1)} %get-tuple-element.31.refs_1_.refs_2_, bf16[768,256]{1,0:T(8,128)(2,1)} %copy-done.7, bf16[768,256]{1,0:T(8,128)(2,1)} %copy-done.8, ...), custom_call_target="tpu_custom_call" | custom-call | flops 402653184 | bytes 6291456 | tf_op jit(solution)/shard_map/pallas_call | solution.py:373
  206.7 14.7 %all-to-all-done.3.r_ref = bf16[16,24,2048]{2,1,0:T(8,128)(2,1)S(1)} async-done(((bf16[16,24,2048]{2,1,0:T(8,128)(2,1)}), bf16[16,24,2048]{2,1,0:T(8,128)(2,1)S(1)}, u32[]{:S(2)}, u32[]{:S(2)}) %all-to-all-start.3) | async-done | bytes 1572896 | tf_op jit(solution)/shard_map/all_to_all | solution.py:276
  221.4 6.0 %all-to-all-start.2 = ((bf16[16,8,2048]{2,1,0:T(8,128)(2,1)}), bf16[16,8,2048]{2,1,0:T(8,128)(2,1)S(1)}, u32[]{:S(2)}, u32[]{:S(2)}) async-start(bf16[16,8,2048]{2,1,0:T(8,128)(2,1)} %shard_map.84), calls=%async_computation.2 | async-start | bytes 1048576 | tf_op jit(solution)/shard_map/all_to_all | solution.py:276
  227.8 2.3 collective-permute-start.18
  230.8 3.9 %collective-permute-done.18.over_back = bf16[32,2048]{1,0:T(8,128)(2,1)S(1)} collective-permute-done((bf16[32,2048]{1,0:T(8,128)(2,1)S(1)}, bf16[32,2048]{1,0:T(8,128)(2,1)S(1)}, u32[]{:S(2)}, u32[]{:S(2)}) %collective-permute-start.18) | collective-permute-done | bytes 131104 | tf_op jit(solution)/shard_map/ppermute | solution.py:406
  234.7 3.9 %collective-permute-done.19.over_fwd = bf16[32,2048]{1,0:T(8,128)(2,1)S(1)} collective-permute-done((bf16[32,2048]{1,0:T(8,128)(2,1)S(1)}, bf16[32,2048]{1,0:T(8,128)(2,1)S(1)}, u32[]{:S(2)}, u32[]{:S(2)}) %collective-permute-start.19) | collective-permute-done | bytes 131104 | tf_op jit(solution)/shard_map/ppermute | solution.py:407
  239.4 2.9 %collective-permute-start.21 = (bf16[64,2048]{1,0:T(8,128)(2,1)S(1)}, bf16[64,2048]{1,0:T(8,128)(2,1)S(1)}, u32[]{:S(2)}, u32[]{:S(2)}) collective-permute-start(bf16[64,2048]{1,0:T(8,128)(2,1)S(1)} %get-tuple-element.44), channel_id=1, source_target_pairs={{0,128},{128,4},{4,132},{132,0},{1,129},{129,5},{5,133},{133,1},{2... | collective-permute-start | bytes 786440 | tf_op jit(solution)/shard_map/ppermute | solution.py:415
  242.6 7.7 %collective-permute-done.20 = bf16[64,2048]{1,0:T(8,128)(2,1)S(1)} collective-permute-done((bf16[64,2048]{1,0:T(8,128)(2,1)S(1)}, bf16[64,2048]{1,0:T(8,128)(2,1)S(1)}, u32[]{:S(2)}, u32[]{:S(2)}) %collective-permute-start.20) | collective-permute-done | bytes 262176 | tf_op jit(solution)/shard_map/ppermute | solution.py:414
  (80 shorter events, 14.8 us)
Async XLA Ops:
  1.7 19.2 %collective-permute-start = (bf16[72,2048]{1,0:T(8,128)(2,1)}, bf16[72,2048]{1,0:T(8,128)(2,1)S(1)}, u32[]{:S(2)}, u32[]{:S(2)}) collective-permute-start(bf16[72,2048]{1,0:T(8,128)(2,1)} %pack.1.refs_0_), channel_id=1, source_target_pairs={{128,0},{4,128},{132,4},{0,132},{129,1},{5,129},{133,5},{1,133},{1... | collective-permute-start | bytes 884744 | tf_op jit(solution)/shard_map/ppermute | solution.py:304
  25.0 72.3 %all-to-all-start.1 = ((bf16[16,24,2048]{2,1,0:T(8,128)(2,1)}), bf16[16,24,2048]{2,1,0:T(8,128)(2,1)S(1)}, u32[]{:S(2)}, u32[]{:S(2)}) async-start(bf16[16,24,2048]{2,1,0:T(8,128)(2,1)} %get-tuple-element.27), calls=%async_computation.1 | async-start | bytes 3145728 | tf_op jit(solution)/shard_map/all_to_all | solution.py:276
  35.9 57.1 %collective-permute-start.4 = (bf16[2,256,768]{2,1,0:T(8,128)(2,1)}, bf16[2,256,768]{2,1,0:T(8,128)(2,1)}, u32[]{:S(2)}, u32[]{:S(2)}) collective-permute-start(bf16[2,256,768]{2,1,0:T(8,128)(2,1)} %get-tuple-element.29), channel_id=1, source_target_pairs={{0,128},{128,0},{1,129},{129,1},{2,130},{130,2},{3,131},{131,3},{4... | collective-permute-start | bytes 2359304 | tf_op jit(solution)/shard_map/ppermute | solution.py:323
  38.0 28.6 %collective-permute-start.1 = (bf16[72,2048]{1,0:T(8,128)(2,1)S(1)}, bf16[72,2048]{1,0:T(8,128)(2,1)S(1)}, u32[]{:S(2)}, u32[]{:S(2)}) collective-permute-start(bf16[72,2048]{1,0:T(8,128)(2,1)S(1)} %copy-done.1), channel_id=1, source_target_pairs={{0,128},{128,4},{4,132},{132,0},{1,129},{129,5},{5,133},{133,1},{2... | collective-permute-start | bytes 884744 | tf_op jit(solution)/shard_map/ppermute | solution.py:305
  66.6 26.5 %copy-start.15 = (bf16[72,2048]{1,0:T(8,128)(2,1)}, bf16[72,2048]{1,0:T(8,128)(2,1)S(1)}, u32[]{:S(2)}) copy-start(bf16[72,2048]{1,0:T(8,128)(2,1)S(1)} %collective-permute-done.1.refs_0_) | copy-start | bytes 884740
  66.6 26.4 %collective-permute-start.2 = (bf16[40,2048]{1,0:T(8,128)(2,1)S(1)}, bf16[40,2048]{1,0:T(8,128)(2,1)S(1)}, u32[]{:S(2)}, u32[]{:S(2)}) collective-permute-start(bf16[40,2048]{1,0:T(8,128)(2,1)S(1)} %slice.8), channel_id=1, source_target_pairs={{0,128},{128,4},{4,132},{132,0},{1,129},{129,5},{5,133},{133,1},{2... | collective-permute-start | bytes 491528 | tf_op jit(solution)/shard_map/ppermute | solution.py:332
  70.2 22.9 %collective-permute-start.3 = (bf16[32,2048]{1,0:T(8,128)(2,1)S(1)}, bf16[32,2048]{1,0:T(8,128)(2,1)S(1)}, u32[]{:S(2)}, u32[]{:S(2)}) collective-permute-start(bf16[32,2048]{1,0:T(8,128)(2,1)S(1)} %slice.9), channel_id=1, source_target_pairs={{128,0},{4,128},{132,4},{0,132},{129,1},{5,129},{133,5},{1,133},{1... | collective-permute-start | bytes 393224 | tf_op jit(solution)/shard_map/ppermute | solution.py:333
  72.7 49.9 %collective-permute-start.5 = (bf16[2,256,768]{2,1,0:T(8,128)(2,1)}, bf16[2,256,768]{2,1,0:T(8,128)(2,1)S(1)}, u32[]{:S(2)}, u32[]{:S(2)}) collective-permute-start(bf16[2,256,768]{2,1,0:T(8,128)(2,1)} %get-tuple-element.28.refs_0_), channel_id=1, source_target_pairs={{0,64},{64,0},{1,65},{65,1},{2,66},{66,2},{3,67},{67,3},{4,68},{68... | collective-permute-start | bytes 2359304 | tf_op jit(solution)/shard_map/ppermute | solution.py:324
  93.0 46.6 %collective-permute-start.6 = (bf16[2,256,768]{2,1,0:T(8,128)(2,1)}, bf16[2,256,768]{2,1,0:T(8,128)(2,1)}, u32[]{:S(2)}, u32[]{:S(2)}) collective-permute-start(bf16[2,256,768]{2,1,0:T(8,128)(2,1)} %collective-permute-done.4.refs_1_), channel_id=1, source_target_pairs={{0,64},{64,0},{1,65},{65,1},{2,66},{66,2},{3,67},{67,3},{4,68},{68... | collective-permute-start | bytes 2359304 | tf_op jit(solution)/shard_map/ppermute | solution.py:325
  98.6 56.9 %all-to-all-start = ((bf16[16,24,2048]{2,1,0:T(8,128)(2,1)}), bf16[16,24,2048]{2,1,0:T(8,128)(2,1)}, u32[]{:S(2)}, u32[]{:S(2)}) async-start(bf16[16,24,2048]{2,1,0:T(8,128)(2,1)} %get-tuple-element.26), calls=%async_computation | async-start | bytes 3145728 | tf_op jit(solution)/shard_map/all_to_all | solution.py:276
  106.0 30.5 %collective-permute-start.11 = (bf16[768,256]{1,0:T(8,128)(2,1)S(1)}, bf16[768,256]{1,0:T(8,128)(2,1)S(1)}, u32[]{:S(2)}, u32[]{:S(2)}) collective-permute-start(bf16[768,256]{1,0:T(8,128)(2,1)S(1)} %copy-done.18), channel_id=1, source_target_pairs={{0,128},{128,0},{1,129},{129,1},{2,130},{130,2},{3,131},{131,3},{4... | collective-permute-start | bytes 1179656 | tf_op jit(solution)/shard_map/ppermute | solution.py:323
  106.1 40.9 %collective-permute-start.7 = (bf16[2,256,768]{2,1,0:T(8,128)(2,1)S(1)}, bf16[2,256,768]{2,1,0:T(8,128)(2,1)}, u32[]{:S(2)}, u32[]{:S(2)}) collective-permute-start(bf16[2,256,768]{2,1,0:T(8,128)(2,1)S(1)} %copy-done.16), channel_id=1, source_target_pairs={{0,32},{32,0},{1,33},{33,1},{2,34},{34,2},{3,35},{35,3},{4,36},{36... | collective-permute-start | bytes 2359304 | tf_op jit(solution)/shard_map/ppermute | solution.py:326
  106.2 39.2 %collective-permute-start.12 = (bf16[768,256]{1,0:T(8,128)(2,1)S(1)}, bf16[768,256]{1,0:T(8,128)(2,1)S(1)}, u32[]{:S(2)}, u32[]{:S(2)}) collective-permute-start(bf16[768,256]{1,0:T(8,128)(2,1)S(1)} %copy-done.6), channel_id=1, source_target_pairs={{0,64},{64,0},{1,65},{65,1},{2,66},{66,2},{3,67},{67,3},{4,68},{68... | collective-permute-start | bytes 1179656 | tf_op jit(solution)/shard_map/ppermute | solution.py:324
  122.6 32.1 %copy-start.17 = (bf16[2,256,768]{2,1,0:T(8,128)(2,1)}, bf16[2,256,768]{2,1,0:T(8,128)(2,1)S(1)}, u32[]{:S(2)}) copy-start(bf16[2,256,768]{2,1,0:T(8,128)(2,1)S(1)} %collective-permute-done.5.refs_2_) | copy-start | bytes 2359300
  122.7 32.1 %collective-permute-start.9 = (bf16[2,256,768]{2,1,0:T(8,128)(2,1)S(1)}, bf16[2,256,768]{2,1,0:T(8,128)(2,1)}, u32[]{:S(2)}, u32[]{:S(2)}) collective-permute-start(bf16[2,256,768]{2,1,0:T(8,128)(2,1)S(1)} %collective-permute-done.5.refs_2_), channel_id=1, source_target_pairs={{0,32},{32,0},{1,33},{33,1},{2,34},{34,2},{3,35},{35,3},{4,36},{36... | collective-permute-start | bytes 2359304 | tf_op jit(solution)/shard_map/ppermute | solution.py:326
  136.4 29.0 %copy-start.7 = (bf16[768,256]{1,0:T(8,128)(2,1)}, bf16[768,256]{1,0:T(8,128)(2,1)S(1)}, u32[]{:S(2)}) copy-start(bf16[768,256]{1,0:T(8,128)(2,1)S(1)} %collective-permute-done.11.refs_2_.refs_3_) | copy-start | bytes 1179652
  136.5 18.8 %collective-permute-start.8 = (bf16[2,256,768]{2,1,0:T(8,128)(2,1)}, bf16[2,256,768]{2,1,0:T(8,128)(2,1)}, u32[]{:S(2)}, u32[]{:S(2)}) collective-permute-start(bf16[2,256,768]{2,1,0:T(8,128)(2,1)} %collective-permute-done.4.refs_1_), channel_id=1, source_target_pairs={{0,32},{32,0},{1,33},{33,1},{2,34},{34,2},{3,35},{35,3},{4,36},{36... | collective-permute-start | bytes 2359304 | tf_op jit(solution)/shard_map/ppermute | solution.py:326
  139.6 15.9 %collective-permute-start.10 = (bf16[2,256,768]{2,1,0:T(8,128)(2,1)}, bf16[2,256,768]{2,1,0:T(8,128)(2,1)}, u32[]{:S(2)}, u32[]{:S(2)}) collective-permute-start(bf16[2,256,768]{2,1,0:T(8,128)(2,1)} %collective-permute-done.6.refs_3_), channel_id=1, source_target_pairs={{0,32},{32,0},{1,33},{33,1},{2,34},{34,2},{3,35},{35,3},{4,36},{36... | collective-permute-start | bytes 2359304 | tf_op jit(solution)/shard_map/ppermute | solution.py:326
  145.4 9.3 %collective-permute-start.13 = (bf16[768,256]{1,0:T(8,128)(2,1)S(1)}, bf16[768,256]{1,0:T(8,128)(2,1)S(1)}, u32[]{:S(2)}, u32[]{:S(2)}) collective-permute-start(bf16[768,256]{1,0:T(8,128)(2,1)S(1)} %collective-permute-done.11.refs_2_.refs_3_), channel_id=1, source_target_pairs={{0,64},{64,0},{1,65},{65,1},{2,66},{66,2},{3,67},{67,3},{4,68},{68... | collective-permute-start | bytes 1179656 | tf_op jit(solution)/shard_map/ppermute | solution.py:325
  147.0 18.5 %collective-permute-start.14 = (bf16[768,256]{1,0:T(8,128)(2,1)S(1)}, bf16[768,256]{1,0:T(8,128)(2,1)S(1)}, u32[]{:S(2)}, u32[]{:S(2)}) collective-permute-start(bf16[768,256]{1,0:T(8,128)(2,1)S(1)} %copy-done.6), channel_id=1, source_target_pairs={{0,32},{32,0},{1,33},{33,1},{2,34},{34,2},{3,35},{35,3},{4,36},{36... | collective-permute-start | bytes 1179656 | tf_op jit(solution)/shard_map/ppermute | solution.py:326
  154.7 10.8 %collective-permute-start.15 = (bf16[768,256]{1,0:T(8,128)(2,1)S(1)}, bf16[768,256]{1,0:T(8,128)(2,1)S(1)}, u32[]{:S(2)}, u32[]{:S(2)}) collective-permute-start(bf16[768,256]{1,0:T(8,128)(2,1)S(1)} %collective-permute-done.11.refs_2_.refs_3_), channel_id=1, source_target_pairs={{0,32},{32,0},{1,33},{33,1},{2,34},{34,2},{3,35},{35,3},{4,36},{36... | collective-permute-start | bytes 1179656 | tf_op jit(solution)/shard_map/ppermute | solution.py:326
  154.7 10.8 %collective-permute-start.16 = (bf16[768,256]{1,0:T(8,128)(2,1)S(1)}, bf16[768,256]{1,0:T(8,128)(2,1)S(1)}, u32[]{:S(2)}, u32[]{:S(2)}) collective-permute-start(bf16[768,256]{1,0:T(8,128)(2,1)S(1)} %collective-permute-done.12.refs_3_.refs_4_), channel_id=1, source_target_pairs={{0,32},{32,0},{1,33},{33,1},{2,34},{34,2},{3,35},{35,3},{4,36},{36... | collective-permute-start | bytes 1179656 | tf_op jit(solution)/shard_map/ppermute | solution.py:326
  155.2 10.3 %collective-permute-start.17 = (bf16[768,256]{1,0:T(8,128)(2,1)S(1)}, bf16[768,256]{1,0:T(8,128)(2,1)S(1)}, u32[]{:S(2)}, u32[]{:S(2)}) collective-permute-start(bf16[768,256]{1,0:T(8,128)(2,1)S(1)} %collective-permute-done.13.refs_4_.refs_5_), channel_id=1, source_target_pairs={{0,32},{32,0},{1,33},{33,1},{2,34},{34,2},{3,35},{35,3},{4,36},{36... | collective-permute-start | bytes 1179656 | tf_op jit(solution)/shard_map/ppermute | solution.py:326
  172.2 22.7 %all-to-all-start.4 = ((bf16[16,16,2048]{2,1,0:T(8,128)(2,1)}), bf16[16,16,2048]{2,1,0:T(8,128)(2,1)S(1)}, u32[]{:S(2)}, u32[]{:S(2)}) async-start(bf16[16,16,2048]{2,1,0:T(8,128)(2,1)} %shard_map.86), calls=%async_computation.4 | async-start | bytes 2097152 | tf_op jit(solution)/shard_map/all_to_all | solution.py:276
  194.9 26.5 %all-to-all-start.3 = ((bf16[16,24,2048]{2,1,0:T(8,128)(2,1)}), bf16[16,24,2048]{2,1,0:T(8,128)(2,1)S(1)}, u32[]{:S(2)}, u32[]{:S(2)}) async-start(bf16[16,24,2048]{2,1,0:T(8,128)(2,1)} %shard_map.85), calls=%async_computation.3 | async-start | bytes 3145728 | tf_op jit(solution)/shard_map/all_to_all | solution.py:276
  201.3 26.1 %copy-start.2 = (bf16[2,128,256]{2,1,0:T(8,128)(2,1)S(1)}, bf16[2,128,256]{2,1,0:T(8,128)(2,1)}, u32[]{:S(2)}) copy-start(bf16[2,128,256]{2,1,0:T(8,128)(2,1)} %get-tuple-element.37.f_ref) | copy-start | bytes 393220
  206.7 31.9 %copy-start.3 = (bf16[2,64,128]{2,1,0:T(8,128)(2,1)S(1)}, bf16[2,64,128]{2,1,0:T(8,128)(2,1)}, u32[]{:S(2)}) copy-start(bf16[2,64,128]{2,1,0:T(8,128)(2,1)} %get-tuple-element.33.f_one) | copy-start | bytes 98308
  221.4 20.9 %all-to-all-start.2 = ((bf16[16,8,2048]{2,1,0:T(8,128)(2,1)}), bf16[16,8,2048]{2,1,0:T(8,128)(2,1)S(1)}, u32[]{:S(2)}, u32[]{:S(2)}) async-start(bf16[16,8,2048]{2,1,0:T(8,128)(2,1)} %shard_map.84), calls=%async_computation.2 | async-start | bytes 1048576 | tf_op jit(solution)/shard_map/all_to_all | solution.py:276
  227.8 6.9 %collective-permute-start.18 = (bf16[32,2048]{1,0:T(8,128)(2,1)S(1)}, bf16[32,2048]{1,0:T(8,128)(2,1)S(1)}, u32[]{:S(2)}, u32[]{:S(2)}) collective-permute-start(bf16[32,2048]{1,0:T(8,128)(2,1)S(1)} %get-tuple-element.40), channel_id=1, source_target_pairs={{128,0},{4,128},{132,4},{0,132},{129,1},{5,129},{133,5},{1,133},{1... | collective-permute-start | bytes 393224 | tf_op jit(solution)/shard_map/ppermute | solution.py:406
  230.1 8.4 %collective-permute-start.19 = (bf16[32,2048]{1,0:T(8,128)(2,1)S(1)}, bf16[32,2048]{1,0:T(8,128)(2,1)S(1)}, u32[]{:S(2)}, u32[]{:S(2)}) collective-permute-start(bf16[32,2048]{1,0:T(8,128)(2,1)S(1)} %get-tuple-element.41), channel_id=1, source_target_pairs={{0,128},{128,4},{4,132},{132,0},{1,129},{129,5},{5,133},{133,1},{2... | collective-permute-start | bytes 393224 | tf_op jit(solution)/shard_map/ppermute | solution.py:407
  239.3 11.0 %collective-permute-start.20 = (bf16[64,2048]{1,0:T(8,128)(2,1)S(1)}, bf16[64,2048]{1,0:T(8,128)(2,1)S(1)}, u32[]{:S(2)}, u32[]{:S(2)}) collective-permute-start(bf16[64,2048]{1,0:T(8,128)(2,1)S(1)} %get-tuple-element.43), channel_id=1, source_target_pairs={{128,0},{4,128},{132,4},{0,132},{129,1},{5,129},{133,5},{1,133},{1... | collective-permute-start | bytes 786440 | tf_op jit(solution)/shard_map/ppermute | solution.py:414
  239.4 12.1 %collective-permute-start.21 = (bf16[64,2048]{1,0:T(8,128)(2,1)S(1)}, bf16[64,2048]{1,0:T(8,128)(2,1)S(1)}, u32[]{:S(2)}, u32[]{:S(2)}) collective-permute-start(bf16[64,2048]{1,0:T(8,128)(2,1)S(1)} %get-tuple-element.44), channel_id=1, source_target_pairs={{0,128},{128,4},{4,132},{132,0},{1,129},{129,5},{5,133},{133,1},{2... | collective-permute-start | bytes 786440 | tf_op jit(solution)/shard_map/ppermute | solution.py:415
  (16 other events, 83.0 us)
